TPU v7x, 32 devices: a whole 2x2x4 slice. The times are simulated.
32 devices in a mesh: dp: 8 (over z, y), mp: 4 (over x, core).
Axes of the slice: x: 2, y: 2, z: 4, core: 2. Of those that a mesh axis runs over, the one named last changes fastest.
Arguments:
- layer_input: bfloat16 [8192, 768], P(('dp', 'mp')), may hold values from -6 to 6
- doc_ids: int32 [8192], P('dp'), may hold values from 0 to 8191, as said below
- type_ids: int32 [8192], P('dp'), may hold values from 0 to 1, as said below
- positions: int32 [8192], P('dp'), may hold values from 0 to 799, as said below
- query_weight: bfloat16 [768, 768], P('dp', 'mp'), may hold values from -0.21875 to 0.21875
- key_weight: bfloat16 [768, 768], P('dp', 'mp'), may hold values from -0.21875 to 0.21875
- value_weight: bfloat16 [768, 768], P('dp', 'mp'), may hold values from -0.21875 to 0.21875
- pos_kernel: bfloat16 [768, 768], P('dp', 'mp'), may hold values from -0.21875 to 0.21875
- out_weight: bfloat16 [768, 768], P('mp', 'dp'), may hold values from -1.25 to 1.25
- inner_weight: bfloat16 [768, 3072], P('dp', 'mp'), may hold values from -0.21875 to 0.21875
- outer_weight: bfloat16 [3072, 768], P('mp', 'dp'), may hold values from -0.109375 to 0.109375
- content_bias: float32 [12, 64], P('mp'), may hold values from -3 to 3
- pos_bias: float32 [12, 64], P('mp'), may hold values from -3 to 3
- type_bias: float32 [12, 64], P('mp'), may hold values from -3 to 3
- value_bias: float32 [12, 64], P('mp'), may hold values from -1.2 to 1.2
- type_embed: float32 [2, 12, 64], P(None, 'mp'), may hold values from -3 to 3
- inner_bias: float32 [3072], P('mp'), may hold values from -3 to 3
- attn_bias: float32 [768], replicated, may hold values from -3 to 3
- ffn_bias: float32 [768], replicated, may hold values from -3 to 3
- attn_gain: float32 [768], replicated, may hold values from 0.5 to 1.5
- attn_shift: float32 [768], replicated, may hold values from -3 to 3
- ffn_gain: float32 [768], replicated, may hold values from 0.5 to 1.5
- ffn_shift: float32 [768], replicated, may hold values from -3 to 3
- out_grad: bfloat16 [8192, 768], P(('dp', 'mp')), may hold values from -6 to 6
Outputs:
- layer_output: bfloat16 [8192, 768], P(('dp', 'mp'))
- input_grad: bfloat16 [8192, 768], P(('dp', 'mp'))
- query_weight_grad: float32 [768, 768], P('dp', 'mp')
- key_weight_grad: float32 [768, 768], P('dp', 'mp')
- value_weight_grad: float32 [768, 768], P('dp', 'mp')
- pos_kernel_grad: float32 [768, 768], P('dp', 'mp')
- out_weight_grad: float32 [768, 768], P('mp', 'dp')
- inner_weight_grad: float32 [768, 3072], P('dp', 'mp')
- outer_weight_grad: float32 [3072, 768], P('mp', 'dp')
- content_bias_grad: float32 [12, 64], P('mp')
- pos_bias_grad: float32 [12, 64], P('mp')
- type_bias_grad: float32 [12, 64], P('mp')
- value_bias_grad: float32 [12, 64], P('mp')
- type_embed_grad: float32 [2, 12, 64], P(None, 'mp')
- inner_bias_grad: float32 [3072], P('mp')
- attn_bias_grad: float32 [768], replicated
- ffn_bias_grad: float32 [768], replicated
- attn_gain_grad: float32 [768], replicated
- attn_shift_grad: float32 [768], replicated
- ffn_gain_grad: float32 [768], replicated
- ffn_shift_grad: float32 [768], replicated
Inputs may be any that keep to these rules, and one draw needn't show every extreme that they name: `doc_ids`: a document's id is the index, among all tokens, of its last token, so ids never fall along the tokens; a document never crosses the boundary of a sequence of 1024 tokens; each document holds at most 800 tokens, and at least 60 unless it ends a sequence; some document holds exactly 800. `type_ids`: within each document, type 0 up to a point and type 1 from there. `positions`: a token's place within its document, counted from 0.
All inputs are finite; a program needn't handle non-finite values.
Results may differ from a plain program's by a relative error of at most 0.034.
Values may be sent and summed in bfloat16 or wider, within the bound.
A program may use at most 128 MiB of HBM per device.

v0:
```python
import functools
import math

import jax
import jax.numpy as jnp
import numpy as np
from jax import lax
from jax.experimental import pallas as pl
from jax.experimental.pallas import tpu as pltpu
from jax.sharding import PartitionSpec as P

f32 = jnp.float32
bf16 = jnp.bfloat16
MESH = pl.DeviceIdType.MESH
MASK = -1e30
DOC_LEAST = 60
NN = (((1,), (0,)), ((), ()))
NT = (((1,), (1,)), ((), ()))
TN = (((0,), (0,)), ((), ()))


def mm(a, b, dims):
    return lax.dot_general(a, b, dims, preferred_element_type=f32)


def lane_of(rows):
    return lax.broadcasted_iota(jnp.int32, (rows, 128), 1)


def low_half(value):
    return jnp.where(lane_of(value.shape[0]) < 64, value, 0.0)


def swap(value):
    return pltpu.roll(value, 64, 1)


class Links:
    def __init__(self, send_sems, recv_sems):
        self.send_sems = send_sems
        self.recv_sems = recv_sems
        self.used = 0
        self.sent = []

    def start(self, src, dst, where):
        copy = pltpu.make_async_remote_copy(
            src_ref=src,
            dst_ref=dst,
            send_sem=self.send_sems.at[self.used],
            recv_sem=self.recv_sems.at[self.used],
            device_id=where,
            device_id_type=MESH,
        )
        self.used += 1
        self.sent.append(copy)
        copy.start()
        return copy

    def drain(self, some=None):
        for copy in some or self.sent:
            copy.wait_send()
            self.sent = [other for other in self.sent if other is not copy]


def norm_stats(summed):
    center = summed - jnp.mean(summed, axis=-1, keepdims=True)
    spread = jnp.mean(center * center, axis=-1, keepdims=True)
    inv_std = lax.rsqrt(spread + 1e-06)
    return center * inv_std, inv_std


def norm_back(grad, normed, inv_std, gain):
    scaled = grad * gain
    return inv_std * (
        scaled
        - jnp.mean(scaled, axis=-1, keepdims=True)
        - normed * jnp.mean(scaled * normed, axis=-1, keepdims=True)
    )


def col_sum(value):
    return jnp.sum(value, axis=0, keepdims=True)


class Ring:
    def __init__(self, count):
        mine = lax.axis_index("dp")
        row = lax.rem(mine, 2)
        along = lax.div(mine, 2)
        self.count = count
        self.place = (1 - row) * along + row * (count - 1 - along)

    def at(self, offset):
        place = lax.rem(self.place + (offset + self.count), self.count)
        back = lax.div(place, self.count // 2)
        return (1 - back) * 2 * place + back * (2 * (self.count - 1 - place) + 1)


class Flow:
    def __init__(self, sign, hops, rows, slot):
        self.sign, self.hops, self.rows, self.slot = sign, hops, rows, slot


def flows_of(count, rows):
    near = count // 2 - 1
    if rows % 32:
        return [Flow(1, near + 1, pl.ds(0, rows), 0), Flow(-1, near, pl.ds(0, rows), near + 1)]
    first, second = pl.ds(0, rows // 2), pl.ds(rows // 2, rows // 2)
    return [
        Flow(1, near + 1, first, 0),
        Flow(-1, near + 1, second, near),
        Flow(-1, near, first, near + 1),
        Flow(1, near, second, 0),
    ]


class Spread:
    def __init__(self, links, ring, bufs):
        self.links, self.ring, self.bufs = links, ring, bufs
        self.done = 0
        self.last = max(f.hops for f in flows_of(ring.count, bufs[0].shape[1]))
        self.moves = {}

    def begin(self):
        self.send(0)

    def send(self, s):
        for b, buf in enumerate(self.bufs):
            for f, flow in enumerate(flows_of(self.ring.count, buf.shape[1])):
                if s > 0 and s <= flow.hops:
                    self.moves[b, f].wait_recv()
                if s < flow.hops:
                    ref = buf.at[self.ring.at(-flow.sign * s), flow.rows]
                    self.moves[b, f] = self.links.start(ref, ref, {"dp": self.ring.at(flow.sign)})

    def step(self):
        if self.done < self.last:
            self.done += 1
            self.send(self.done)

    def finish(self):
        while self.done < self.last:
            self.step()


class Collect:
    def __init__(self, links, ring, bufs, gots):
        self.links, self.ring = links, ring
        self.bufs, self.gots = bufs, gots
        self.done = 0
        self.last = max(f.hops for f in flows_of(ring.count, bufs[0].shape[1]))
        self.moves = {}

    def begin(self):
        self.send(0)

    def send(self, s):
        for b, (buf, got) in enumerate(zip(self.bufs, self.gots)):
            for f, flow in enumerate(flows_of(self.ring.count, buf.shape[1])):
                if s > 0 and s <= flow.hops:
                    self.moves[b, f].wait_recv()
                if s < flow.hops:
                    owner = self.ring.at(flow.sign * (flow.hops - s))
                    if s > 0:
                        both = buf[owner, flow.rows].astype(f32) + got[flow.slot + s - 1, flow.rows].astype(f32)
                        buf[owner, flow.rows] = both.astype(bf16)
                    self.moves[b, f] = self.links.start(
                        buf.at[owner, flow.rows], got.at[flow.slot + s, flow.rows], {"dp": self.ring.at(flow.sign)}
                    )

    def step(self):
        if self.done < self.last:
            self.done += 1
            self.send(self.done)

    def finish(self):
        while self.done < self.last:
            self.step()

    def take(self, b, out_ref, columns):
        buf, got = self.bufs[b], self.gots[b]
        mine = self.ring.at(0)
        flows = flows_of(self.ring.count, buf.shape[1])
        for start in sorted({flow.rows.start for flow in flows}):
            total = None
            for flow in flows:
                if flow.rows.start == start:
                    part = got[flow.slot + flow.hops - 1, flow.rows].astype(f32)
                    total = buf[mine, flow.rows].astype(f32) + part if total is None else total + part
                    rows = flow.rows
            out_ref[rows, columns] = total


IN_BOTH = (
    "x_ref", "og_ref", "doc_ref", "kind_ref", "cb_ref", "pb_ref", "tbias_ref", "vb_ref", "te_ref", "ib_ref", "ab_ref",
    "fb_ref", "ag_ref", "as_ref", "fg_ref", "fs_ref", "ta_ref", "tb_ref",
)
IN_RING = (
    "wq_ref", "wk_ref", "wv_ref", "wp_ref", "wo_ref", "wi_ref", "wu_ref",
)
IN_WHOLE = (
    "w1g", "wog", "wig", "wug",
)
OUT_WHOLE = (
    "dwa", "dwb", "dwo", "dwi", "dwu",
)


def layer_kernel(ring_on, names, *refs):
    r = dict(zip(names, refs, strict=True))
    (x_ref, og_ref, doc_ref, kind_ref, cb_ref, pb_ref, tbias_ref, vb_ref, te_ref, ib_ref,
     ab_ref, fb_ref, ag_ref, as_ref, fg_ref, fs_ref, ta_ref, tb_ref) = (r[n] for n in IN_BOTH)
    w1g, wog, wig, wug = (r[n] for n in IN_WHOLE)
    dwa, dwb, dwo, dwi, dwu = (r[n] for n in OUT_WHOLE)
    out_ref, ig_ref = r["out_ref"], r["ig_ref"]
    vec_ref, hs_ref = r["vec"], r["hs"]
    (xs, hb, eb2, eb1, part_a, part_b, r1a, r1b, r2a, r2b, sxa, sxb, own_f,
     table, rel, qa, qr, ka, va, q32, es, a32, attnp, act, slope, igr,
     h1, n1, e2, inv1, e1, dkv, drt, dqkv, flip, qmeta_ref, kmeta_ref, small_ref, per_head, ln_ref, ibs,
     send_sems, recv_sems) = (r[n] for n in SCRATCH)
    rows = x_ref.shape[0]
    width = x_ref.shape[1]
    hidden = wig.shape[2]
    members = xs.shape[0]
    seq = members * rows
    heads = es.shape[0]
    half = width // 2
    scale = 0.125
    me = lax.axis_index("mp")
    core = lax.rem(me, 2)
    side = lax.div(me, 2)
    mate = me + 1 - 2 * core
    across = lax.rem(me + 2, 4)
    diag = lax.rem(mate + 2, 4)
    links = Links(send_sems, recv_sems)
    to_mate = {"mp": mate}
    to_across = {"mp": across}

    barrier = pltpu.get_barrier_semaphore()
    peers = [to_mate, to_across]
    if ring_on:
        ring = Ring(w1g.shape[0])
        peers += [{"dp": ring.at(1)}, {"dp": ring.at(-1)}]
    for where in peers:
        pl.semaphore_signal(barrier, inc=1, device_id=where, device_id_type=MESH)
    pl.semaphore_wait(barrier, len(peers))

    def whole(ref):
        return ref[...].reshape(width, ref.shape[2])

    def gather_start(buf):
        a = links.start(buf.at[me], buf.at[me], to_across)
        b = links.start(buf.at[me], buf.at[me], to_mate)
        return a, b

    def gather_forward(buf, first):
        first.wait_recv()
        return links.start(buf.at[across], buf.at[across], to_mate)

    part_rows = rows // 2
    halves = [pl.ds(0, part_rows), pl.ds(part_rows, part_rows)]
    near_pair, far_pair = pl.ds(2 * side, 2), pl.ds(2 * (1 - side), 2)

    class Gather:
        def __init__(self, buf, x):
            self.buf, self.x = buf, x
            mine_x = buf.at[me, halves[x]]
            self.over = links.start(mine_x, mine_x, to_across)
            self.beside = links.start(mine_x, mine_x, to_mate)

        def forward(self):
            self.over.wait_recv()
            theirs = self.buf.at[across, halves[self.x]]
            self.last = links.start(theirs, theirs, to_mate)

    xs[me] = x_ref[...]
    x_a, x_b = gather_start(xs)

    if ring_on:
        shard = w1g.shape[1]
        mine = ring.at(0)
        own_f[...] = jnp.zeros(own_f.shape, f32)
        tiles = []
        for i, name in enumerate(IN_RING[:4]):
            r0, c0 = 128 * (i // 2), 256 * (i % 2)
            own_f[r0 : r0 + shard, c0 : c0 + r[name].shape[1]] = r[name][...].astype(f32)
            tiles.append((own_f[r0 : r0 + shard, c0 : c0 + 128], own_f[r0 : r0 + shard, c0 + 128 : c0 + 256]))
        (qx, qy), (kx, ky), (vx, vy), (px, py) = tiles
        low = lane_of(shard) < 64
        joined = [
            jnp.where(low, kx, swap(vx)),
            jnp.where(low, swap(kx), vx),
            jnp.where(low, ky, swap(vy)),
            qx,
            jnp.where(low, qy, swap(px)),
            jnp.where(low, swap(px), swap(py)),
        ]
        for i, tile in enumerate(joined):
            w1g[mine, :, 128 * i : 128 * i + 128] = tile.astype(bf16)
        spread_1 = Spread(links, ring, [w1g])
        spread_1.begin()
        wo_ref = r["wo_ref"]
        own_f[:, :128] = jnp.zeros((256, 128), f32)
        own_f[: wo_ref.shape[0], :shard] = wo_ref[...].astype(f32)
        wog[mine] = jnp.transpose(own_f[:, :128], (1, 0))[:shard].astype(bf16)
        wig[mine] = r["wi_ref"][...]
        wug[mine] = r["wu_ref"][...]
        spread_o, spread_i, spread_u = (Spread(links, ring, [ref]) for ref in (wog, wig, wug))

    small_ref[...] = jnp.zeros(small_ref.shape, f32)
    for h in range(heads):
        for i, ref in enumerate((cb_ref, pb_ref, tbias_ref)):
            small_ref[h, i : i + 1, 0:64] = ref[h : h + 1, :]
        small_ref[h, 3:5, 0:64] = te_ref[h]
        small_ref[h, 5:6, 0:64] = vb_ref[h : h + 1, :]
    for i, ref in enumerate((ab_ref, ag_ref, as_ref, fb_ref, fg_ref, fs_ref)):
        ln_ref[i : i + 1, :] = ref[...].reshape(1, width)
    ibs[0:1, :] = ib_ref[...].reshape(1, hidden)

    slots = seq // DOC_LEAST + 2
    ends = (doc_ref[...].reshape(1, seq) - lax.axis_index("dp") * seq).astype(f32)
    slot = jnp.where(ends > seq - 1.5, slots - 1.0, jnp.floor((ends + 0.5) * (1.0 / DOC_LEAST)))
    slot = jnp.transpose(jnp.broadcast_to(slot, (128, seq)), (1, 0))
    kind = jnp.transpose(jnp.broadcast_to(kind_ref[...].reshape(1, seq).astype(f32), (128, seq)), (1, 0))
    lane = lane_of(seq)
    hit = jnp.abs(slot + 68.0 - lane.astype(f32)) < 0.5
    qmeta_ref[...] = jnp.where(lane == 64, kind, jnp.where(hit, 1.0, 0.0)).astype(bf16)
    miss = jnp.where(hit, 0.0, MASK)
    kmeta_ref[...] = jnp.where(
        lane < 66, 1.0, jnp.where(lane < 68, kind, jnp.where(lane < 68 + slots, miss, 0.0))
    ).astype(bf16)
    x_f = gather_forward(xs, x_a)
    if ring_on:
        spread_1.step()

    steps = tb_ref.shape[1]

    def table_step(u, carry):
        sa = ta_ref[0, pl.ds(u, 1), :]
        ca = ta_ref[1, pl.ds(u, 1), :]
        at = pl.multiple_of(u * steps, steps)
        table[pl.ds(at, steps), :half] = (sa * tb_ref[1] - ca * tb_ref[0]).astype(bf16)
        table[pl.ds(at, steps), half:] = (ca * tb_ref[1] + sa * tb_ref[0]).astype(bf16)
        return carry

    lax.fori_loop(0, ta_ref.shape[1] // 2, table_step, 0)
    if ring_on:
        spread_1.step()
    lax.fori_loop(ta_ref.shape[1] // 2, ta_ref.shape[1], table_step, 0)

    ri = lax.broadcasted_iota(jnp.int32, (rows, rows), 0)
    ci = lax.broadcasted_iota(jnp.int32, (rows, rows), 1)
    flip[...] = jnp.where(ri + ci == rows - 1, 1.0, 0.0).astype(bf16)
    if ring_on:
        spread_1.step()
        spread_o.begin()
        spread_1.finish()

    def rel_step(i, carry):
        at = pl.ds(pl.multiple_of(i * 256, 256), 256)
        got = mm(table[at, :], w1g[:, :, 512:768].reshape(width, 256), NN)
        rel[0, at, :] = low_half(swap(got[:, :128])).astype(bf16)
        rel[1, at, :] = low_half(got[:, 128:]).astype(bf16)
        rel[2, at, :] = low_half(swap(got[:, 128:])).astype(bf16)
        return carry

    lax.fori_loop(0, 2 * seq // 256, rel_step, 0)

    def project(o, carry):
        at = pl.ds(pl.multiple_of(o * rows, rows), rows)
        got = mm(xs[o], w1g[:, :, :640].reshape(width, 640), NN)
        lane = lane_of(rows)
        qmeta = qmeta_ref[at, :].astype(f32)
        kmeta = kmeta_ref[at, :].astype(f32)
        typed = qmeta[:, 64:65]
        for h in range(heads):
            kv = got[:, 128 * h : 128 * h + 128]
            ka[h, at, :] = jnp.where(lane < 64, kv, kmeta).astype(bf16)
            vrow = swap(kv) + small_ref[h, 5:6, :]
            va[h, at, :] = jnp.where(lane < 64, vrow, jnp.where(lane < 66, 1.0, 0.0)).astype(bf16)
            q = got[:, 384:512] if h < 2 else got[:, 512:640]
            if h == 1:
                q = swap(q)
            q = low_half(q)
            q32[h, at, :] = q
            qt = q + small_ref[h, 2:3, :]
            ct0 = jnp.sum(qt * small_ref[h, 3:4, :], axis=1, keepdims=True)
            ct1 = jnp.sum(qt * small_ref[h, 4:5, :], axis=1, keepdims=True)
            diff = (ct1 - ct0) * scale
            base = ct0 * scale + diff * (1.0 - typed)
            tilt = diff * (2.0 * typed - 1.0)
            base_hi = base.astype(bf16).astype(f32)
            tilt_hi = tilt.astype(bf16).astype(f32)
            extra = jnp.where(
                lane == 64,
                base_hi,
                jnp.where(
                    lane == 65,
                    base - base_hi,
                    jnp.where(lane == 66, tilt_hi, jnp.where(lane == 67, tilt - tilt_hi, qmeta)),
                ),
            )
            qc = (q + small_ref[h, 0:1, :]) * scale
            qa[h, at, :] = jnp.where(lane < 64, qc, extra).astype(bf16)
            qr[h, at, :] = low_half((q + small_ref[h, 1:2, :]) * scale).astype(bf16)
        return carry

    def poll(*steppers):
        for stepper in steppers:
            stepper.step()

    if ring_on:
        spread_o.step()
    x_b.wait_recv()
    x_f.wait_recv()
    lax.fori_loop(0, members, project, 0)
    if ring_on:
        poll(spread_o)
        spread_i.begin()

    wide = seq + rows

    def attend(o, between=None):
        at = pl.ds(pl.multiple_of(o * rows, rows), rows)
        window = pl.ds(pl.multiple_of((members - 1 - o) * rows, rows), wide)

        def one_head(h, carry):
            s = mm(qa[h, at, :], ka[h], NT)
            g = mm(qr[h, at, :], rel[h, window, :], NT)
            g = pltpu.roll(g, wide + 1 - rows, 1, stride=1, stride_axis=0)
            s = s + g[:, :seq]
            top = jnp.max(s, axis=1, keepdims=True)
            e = jnp.exp(s - top).astype(bf16)
            es[h, at, :] = e
            o_full = mm(e, va[h], NN)
            inv = 1.0 / o_full[:, 64:65]
            a32[h, at, :] = jnp.where(lane_of(rows) < 64, o_full * inv, inv)
            return carry

        if between:
            lax.fori_loop(0, 1, one_head, 0)
            between()
        lax.fori_loop(1 if between else 0, heads, one_head, 0)
        first = low_half(a32[0, at, :]) + swap(low_half(a32[1, at, :]))
        attnp[at, :128] = first.astype(bf16)
        attnp[at, 128:] = low_half(a32[2, at, :]).astype(bf16)

    def branch_of(o):
        return mm(attnp[pl.ds(pl.multiple_of(o * rows, rows), rows), :], whole(wog), NT)

    class Scatter:
        def __init__(self, part, r1, r2, sx):
            self.part, self.r1, self.r2, self.sx = part, r1, r2, sx
            self.far, self.near, self.over = [None, None], [None, None], [None, None]

        def give_diag(self, x, value):
            self.part[diag, halves[x]] = value.astype(bf16)
            self.far[x] = links.start(self.part.at[diag, halves[x]], self.r1.at[1 - side, halves[x]], to_mate)

        def give_across(self, x, value):
            self.part[across, halves[x]] = value.astype(bf16)

        def give_mate(self, x, value):
            self.part[mate, halves[x]] = value.astype(bf16)
            self.near[x] = links.start(self.part.at[mate, halves[x]], self.r1.at[side, halves[x]], to_mate)

        def give_own(self, x, value):
            own_f[halves[x]] = value

        def give_near(self, x, pair):
            self.give_mate(x, jnp.where(core == 0, pair[1], pair[0]))
            self.give_own(x, jnp.where(core == 0, pair[0], pair[1]))

        def give_far(self, x, pair):
            self.give_diag(x, jnp.where(core == 0, pair[1], pair[0]))
            self.give_across(x, jnp.where(core == 0, pair[0], pair[1]))

        def pass_on(self, x):
            self.far[x].wait_recv()
            both = self.part[across, halves[x]].astype(f32) + self.r1[1 - side, halves[x]].astype(f32)
            self.sx[halves[x]] = both.astype(bf16)
            self.over[x] = links.start(self.sx.at[halves[x]], self.r2.at[halves[x]], to_across)

        def release(self):
            links.drain(self.far + self.near + self.over)

        def take(self, x):
            self.near[x].wait_recv()
            near = own_f[halves[x]] + self.r1[side, halves[x]].astype(f32)
            self.over[x].wait_recv()
            return near + self.r2[halves[x]].astype(f32)

    def split(value):
        return value[:part_rows], value[part_rows:]

    first_red = red = Scatter(part_a, r1a, r2a, sxa)
    attend(diag)
    if ring_on:
        poll(spread_o, spread_i)
        spread_u.begin()
    attend(across)
    if ring_on:
        spread_o.finish()
    for x, (there, here) in enumerate(zip(split(branch_of(diag)), split(branch_of(across)))):
        red.give_diag(x, there)
        red.give_across(x, here)
    if ring_on:
        poll(spread_i, spread_u)

    def first_pass():
        red.pass_on(0)
        red.pass_on(1)

    attend(mate, first_pass)
    for x, value in enumerate(split(branch_of(mate))):
        red.give_mate(x, value)
    if ring_on:
        poll(spread_i, spread_u)
    attend(me)
    for x, value in enumerate(split(branch_of(me))):
        red.give_own(x, value)
    vec_ref[...] = jnp.zeros((8, width), f32)
    hs_ref[...] = jnp.zeros(hs_ref.shape, f32)

    def first_norm(x):
        at = halves[x]
        summed = x_ref[at, :].astype(f32) + first_red.take(x) + ln_ref[0:1, :]
        normed, inv_std = norm_stats(summed)
        n1[at, :] = normed
        inv1[at, :] = jnp.broadcast_to(inv_std, (part_rows, 128))
        h1[at, :] = normed * ln_ref[1:2, :] + ln_ref[2:3, :]
        hb[me, at] = h1[at, :].astype(bf16)
        return Gather(hb, x)

    def ffn(pair, x):
        inner = mm(hb[pair, halves[x]].reshape(rows, width), whole(wig), NN) + ibs[0:1, :]
        square = inner * inner
        t = jnp.tanh(0.7978845608028654 * (inner + 0.044715 * square * inner))
        made = (0.5 * inner * (1.0 + t)).astype(bf16)
        act[pair, halves[x]] = made.reshape(2, part_rows, hidden)
        steep = (
            0.5 * (1.0 + t)
            + 0.5 * inner * (1.0 - t * t) * 0.7978845608028654 * (1.0 + 3.0 * 0.044715 * square)
        ).astype(bf16)
        slope[pair, halves[x]] = steep.reshape(2, part_rows, hidden)
        return mm(made, whole(wug), NT).reshape(2, part_rows, width)

    def stage(start, block, reducer, ready=None):
        moves = [start(0), start(1)]
        if ready:
            ready()
        for x in (0, 1):
            moves[x].beside.wait_recv()
            reducer.give_near(x, block(near_pair, x))
        moves[0].forward()
        moves[0].last.wait_recv()
        reducer.give_far(0, block(far_pair, 0))
        moves[1].forward()
        reducer.pass_on(0)
        moves[1].last.wait_recv()
        reducer.give_far(1, block(far_pair, 1))
        reducer.pass_on(1)

    def weights_ready():
        spread_i.finish()
        spread_u.finish()

    if ring_on:
        poll(spread_i, spread_u)
    second_red = red = Scatter(part_b, r1b, r2b, sxb)
    stage(first_norm, ffn, second_red, weights_ready if ring_on else None)

    def second_norm(x):
        at = halves[x]
        summed = h1[at, :] + second_red.take(x) + ln_ref[3:4, :]
        normed, inv_std = norm_stats(summed)
        out_ref[at, :] = (normed * ln_ref[4:5, :] + ln_ref[5:6, :]).astype(bf16)
        grad = og_ref[at, :].astype(f32)
        back = norm_back(grad, normed, inv_std, ln_ref[4:5, :])
        e2[at, :] = back
        eb2[me, at] = back.astype(bf16)
        move = Gather(eb2, x)
        vec_ref[4:5, :] += col_sum(grad * normed)
        vec_ref[5:6, :] += col_sum(grad)
        vec_ref[1:2, :] += col_sum(back)
        return move

    def ffn_back(pair, x):
        steep = slope[pair, halves[x]].reshape(rows, hidden).astype(f32)
        grad_inner = (mm(eb2[pair, halves[x]].reshape(rows, width), whole(wug), NN) * steep).astype(bf16)
        igr[pair, halves[x]] = grad_inner.reshape(2, part_rows, hidden)
        vec_ref[6:7, :hidden] += col_sum(grad_inner.astype(f32))
        return mm(grad_inner, whole(wig), NT).reshape(2, part_rows, width)

    third_red = Scatter(part_a, r1a, r2a, sxa)
    stage(second_norm, ffn_back, third_red, first_red.release)
    flat = lambda ref: ref[...].reshape(seq, ref.shape[2])

    def put(ref, value):
        ref[...] = value.astype(bf16).reshape(ref.shape)

    def third_norm(x):
        at = halves[x]
        grad = e2[at, :] + third_red.take(x)
        back = norm_back(grad, n1[at, :], inv1[at, :1], ln_ref[1:2, :])
        e1[at, :] = back
        eb1[me, at] = back.astype(bf16)
        move = Gather(eb1, x)
        vec_ref[2:3, :] += col_sum(grad * n1[at, :])
        vec_ref[3:4, :] += col_sum(grad)
        vec_ref[0:1, :] += col_sum(back)
        return move

    put(dwu, mm(flat(eb2), flat(act), TN))
    if ring_on:
        collect_u = Collect(links, ring, [dwu], [r["gwu"]])
        collect_u.begin()
    g_0 = third_norm(0)
    put(dwi, mm(flat(hb), flat(igr), TN))
    if ring_on:
        collect_i = Collect(links, ring, [dwi], [r["gwi"]])
        collect_i.begin()
    g_1 = third_norm(1)
    if ring_on:
        vec_all, vec_mp = r["vec_all"], r["vec_mp"]
        vec_all[mine] = vec_ref[...]
        spread_4 = Spread(links, ring, [vec_all])
        spread_4.begin()

    dkv[...] = jnp.zeros(dkv.shape, f32)
    drt[...] = jnp.zeros(drt.shape, f32)

    def attend_back(o):
        at = pl.ds(pl.multiple_of(o * rows, rows), rows)
        lo = pl.multiple_of((members - 1 - o) * rows, rows)
        window = pl.ds(lo, wide)
        d_all = mm(eb1[o], whole(wog), NN).astype(bf16).astype(f32)
        lane = lane_of(rows)
        typed = qmeta_ref[at, :].astype(f32)[:, 64:65]
        per_head[0] = d_all[:, :128]
        per_head[1] = swap(d_all[:, :128])
        per_head[2] = d_all[:, 128:]

        def one_head(h, carry):
            d_out = per_head[h]
            kept = a32[h, at, :]
            d_out = low_half(d_out * kept[:, 64:65]).astype(bf16).astype(f32)
            d_row = -jnp.sum(d_out * kept, axis=1, keepdims=True)
            d_hi = d_row.astype(bf16).astype(f32)
            d_aug = jnp.where(lane == 64, d_hi, jnp.where(lane == 65, d_row - d_hi, d_out)).astype(bf16)
            e = es[h, at, :]
            ds = (e.astype(f32) * mm(d_aug, va[h], NT)).astype(bf16)
            dkv[h, 64:128, :] += mm(d_aug, e, TN)[:64]
            dkv[h, 0:64, :] += mm(qa[h, at, :], ds, TN)[:64]
            dq = mm(ds, ka[h], NN) * scale
            turned = mm(flip[...], ds, NN)
            turned = jnp.concatenate([turned, jnp.zeros((rows, rows), f32)], axis=1)
            dg = pltpu.roll(turned, 0, 1, stride=1, stride_axis=0).astype(bf16)
            dqr = mm(dg, rel[h, window, :], NN) * scale
            qr_turned = mm(flip[...], qr[h, at, :], NN).astype(bf16)
            drt[pl.ds(pl.multiple_of(64 * h + 64, 64), 64), window] += mm(qr_turned, dg, TN)[:64]
            hs_ref[h, 1:2, :] += col_sum(dqr)
            dqr_hi = dqr.astype(bf16)
            dqr_lo = (dqr - dqr_hi.astype(f32)).astype(bf16)
            dqr = mm(flip[...], dqr_hi, NN) + mm(flip[...], dqr_lo, NN)
            total = dq[:, 64:65]
            ones = dq[:, 66:67]
            same = jnp.where(typed > 0.5, ones, total - ones)
            other = total - same
            dqt = other * small_ref[h, 3:4, :] + same * small_ref[h, 4:5, :]
            qt = q32[h, at, :] + small_ref[h, 2:3, :]
            hs_ref[h, 0:1, :] += col_sum(dq)
            hs_ref[h, 2:3, :] += col_sum(dqt)
            hs_ref[h, 3:4, :] += col_sum(other * qt)
            hs_ref[h, 4:5, :] += col_sum(same * qt)
            per_head[h] = low_half(dq + dqr + dqt)
            return carry

        lax.fori_loop(0, heads, one_head, 0)
        dqkv[at, 384:512] = (per_head[0] + swap(per_head[1])).astype(bf16)
        dqkv[at, 512:640] = per_head[2].astype(bf16)

    attend_back(me)
    g_0.beside.wait_recv()
    g_1.beside.wait_recv()
    g_0.forward()
    g_1.forward()
    if ring_on:
        poll(spread_4, collect_u, collect_i)
    attend_back(mate)
    if ring_on:
        poll(spread_4, collect_u, collect_i)
    attend_back(across)
    g_0.last.wait_recv()
    g_1.last.wait_recv()
    put(dwo, mm(flat(eb1), attnp[...], TN))
    if ring_on:
        spread_4.finish()
        total = vec_all[0]
        for i in range(1, ring.count):
            total = total + vec_all[i]
        vec_mp[me] = total
        v_a, v_b = gather_start(vec_mp)
        poll(collect_u, collect_i)
        collect_2 = Collect(links, ring, [dwo], [r["gwo"]])
        collect_2.begin()
    attend_back(diag)
    if ring_on:
        poll(collect_u, collect_i, collect_2)
        v_b.wait_recv()
        v_f = gather_forward(vec_mp, v_a)

    for h in range(heads):
        turned = jnp.transpose(dkv[h], (1, 0)).astype(bf16)
        dqkv[:, 128 * h : 128 * h + 128] = turned
        hs_ref[h, 5:6, :] = swap(col_sum(turned.astype(f32)))
    put(dwa, mm(flat(xs), dqkv[:, :512], TN))
    if ring_on:
        hs_all = r["hs_all"]
        hs_all[mine] = hs_ref[...].reshape(8 * heads, 128)
        spread_5 = Spread(links, ring, [hs_all])
        spread_5.begin()
        collect_3 = Collect(links, ring, [dwa], [r["gwa"]])
        collect_3.begin()

    def input_back(o):
        at = pl.ds(pl.multiple_of(o * rows, rows), rows)
        return mm(dqkv[at, :], w1g[:, :, :640].reshape(width, 640), NT)

    second_red.release()
    red = Scatter(part_b, r1b, r2b, sxb)
    for x, value in enumerate(split(input_back(diag))):
        red.give_diag(x, value)
    for x, value in enumerate(split(input_back(across))):
        red.give_across(x, value)
    tail = mm(flat(xs), dqkv[:, 512:640], TN)
    d_pos = jnp.transpose(mm(drt[...].astype(bf16), table[...], NN), (1, 0))
    put(dwb, jnp.concatenate([tail + d_pos[:, :128], d_pos[:, 128:]], axis=1))
    if ring_on:
        collect_4 = Collect(links, ring, [dwb], [r["gwb"]])
        collect_4.begin()
    red.pass_on(0)
    red.pass_on(1)
    if ring_on:
        poll(collect_2, collect_3, spread_5)
    for x, value in enumerate(split(input_back(mate))):
        red.give_mate(x, value)
    for x, value in enumerate(split(input_back(me))):
        red.give_own(x, value)
    if ring_on:
        grad_ref = r["grad_ref"]
        poll(collect_4, collect_3, spread_5)
        collect_u.finish()
        collect_i.finish()
        collect_u.take(0, grad_ref, pl.ds(1024 + hidden, hidden))
        poll(collect_2)
        collect_i.take(0, grad_ref, pl.ds(1024, hidden))
        poll(collect_4, collect_3, spread_5)
        v_f.wait_recv()
        r["vec_ref"][...] = vec_mp[0] + vec_mp[1] + vec_mp[2] + vec_mp[3]
        r["vec_ref"][6:7, :] = vec_mp[me][6:7, :]
        collect_2.finish()
        collect_2.take(0, grad_ref, pl.ds(768, 256))
        poll(collect_4, collect_3, spread_5)
    for x in (0, 1):
        ig_ref[halves[x], :] = (e1[halves[x], :] + red.take(x)).astype(bf16)
    if ring_on:
        spread_5.finish()
        total = hs_all[0]
        for i in range(1, ring.count):
            total = total + hs_all[i]
        r["hs_ref"][...] = total
        collect_3.finish()
        collect_3.take(0, grad_ref, pl.ds(0, 512))
        collect_4.finish()
        collect_4.take(0, grad_ref, pl.ds(512, 256))
    else:
        r["vec_ref"][...] = vec_ref[...]
        r["hs_ref"][...] = hs_ref[...].reshape(8 * heads, 128)
    links.drain()


SCRATCH = (
    "xs", "hb", "eb2", "eb1", "part_a", "part_b", "r1a", "r1b", "r2a", "r2b", "sxa", "sxb", "own_f", "table", "rel",
    "qa", "qr", "ka", "va", "q32", "es", "a32", "attnp", "act", "slope", "igr", "h1", "n1", "e2", "inv1", "e1", "dkv",
    "drt", "dqkv", "flip", "qmeta", "kmeta", "small", "per_head", "ln", "ibs", "send_sems", "recv_sems",
)


def finish_kernel(
    out_ref, ig_ref, grad_ref, vec_ref, hs_ref,
    out, in_grad, wq, wk, wv, wp, wo, wi, wu, cb, pb, tbias, vb, te, ib, ab, fb, ag, ash, fg, fs, turn,
):
    out[...] = out_ref[...]
    in_grad[...] = ig_ref[...]
    shard, hidden = wi.shape
    t = [grad_ref[:, 128 * i : 128 * i + 128].astype(f32) for i in range(6)]
    low = lane_of(shard) < 64
    wk[:, :128] = jnp.where(low, t[0], swap(t[1]))
    wk[:, 128:] = t[2][:, :64]
    wv[:, :128] = jnp.where(low, swap(t[0]), t[1])
    wv[:, 128:] = swap(t[2])[:, :64]
    wq[:, :128] = t[3]
    wq[:, 128:] = t[4][:, :64]
    wp[:, :128] = jnp.where(low, swap(t[4]), swap(t[5]))
    wp[:, 128:] = swap(t[5])[:, :64]
    turn[...] = jnp.zeros(turn.shape, f32)
    turn[:shard, :] = grad_ref[:, 768:1024].astype(f32)
    wo[...] = jnp.transpose(turn[...], (1, 0))[: wo.shape[0], :shard]
    wi[...] = grad_ref[:, 1024 : 1024 + hidden].astype(f32)
    wu[...] = grad_ref[:, 1024 + hidden :].astype(f32)
    for h in range(cb.shape[0]):
        for i, ref in ((0, cb), (1, pb), (2, tbias), (5, vb)):
            ref[h : h + 1, :] = hs_ref[8 * h + i : 8 * h + i + 1, :64]
        te[h] = hs_ref[8 * h + 3 : 8 * h + 5, :64]
    ib[...] = vec_ref[6:7, :hidden].reshape(hidden)
    for i, ref in enumerate((ab, fb, ag, ash, fg, fs)):
        ref[...] = vec_ref[i : i + 1, :].reshape(ref.shape[0])


def angle_tables(seq, width):
    half = width // 2
    freq = 1.0 / 10000.0 ** (np.arange(half, dtype=np.float64) * (2.0 / width))
    steps = 32
    coarse = (seq - 1 - steps * np.arange(2 * seq // steps, dtype=np.float64))[:, None] * freq[None, :]
    fine = np.arange(steps, dtype=np.float64)[:, None] * freq[None, :]
    return (
        np.stack([np.sin(coarse), np.cos(coarse)]).astype(np.float32),
        np.stack([np.sin(fine), np.cos(fine)]).astype(np.float32),
    )


def per_device(
    layer_input, doc_ids, type_ids, positions, query_weight, key_weight, value_weight, pos_kernel,
    out_weight, inner_weight, outer_weight, content_bias, pos_bias, type_bias, value_bias, type_embed,
    inner_bias, attn_bias, ffn_bias, attn_gain, attn_shift, ffn_gain, ffn_shift, out_grad,
):
    rows, width = layer_input.shape
    seq = doc_ids.shape[0]
    heads, depth = content_bias.shape
    hidden = inner_weight.shape[1]
    shard = query_weight.shape[0]
    members = seq // rows
    count = width // shard
    cols = heads * depth
    ring_on = shard % 16 == 0 and count % 2 == 0 and count > 2

    type_rows = jnp.transpose(type_embed, (1, 0, 2))
    ta, tb = angle_tables(seq, width)
    given = [
        layer_input, out_grad, doc_ids, type_ids, content_bias, pos_bias, type_bias, value_bias, type_rows, inner_bias,
        attn_bias, ffn_bias, attn_gain, attn_shift, ffn_gain, ffn_shift, ta, tb,
    ]
    sds = jax.ShapeDtypeStruct
    vm = pltpu.VMEM
    blocks = count if ring_on else 1
    deep = width // blocks
    full = {
        "w1g": 768, "wog": 256, "wig": hidden, "wug": hidden,
        "dwa": 512, "dwb": 256, "dwo": 256, "dwi": hidden, "dwu": hidden,
    }
    outs = {
        "out_ref": sds((rows, width), bf16), "ig_ref": sds((rows, width), bf16),
        "vec_ref": sds((8, width), f32), "hs_ref": sds((8 * heads, 128), f32),
    }
    extra = {"vec": vm((8, width), f32), "hs": vm((heads, 8, 128), f32)}
    if ring_on:
        given += [query_weight, key_weight, value_weight, pos_kernel, out_weight, inner_weight, outer_weight.T]
        names = IN_BOTH + IN_RING
        outs["grad_ref"] = sds((shard, 1024 + 2 * hidden), f32)
        extra |= {name: vm((blocks, deep, wide), bf16) for name, wide in full.items()}
        for name in OUT_WHOLE:
            extra["g" + name[1:]] = vm((blocks - 1, deep, full[name]), bf16)
        extra["vec_all"] = vm((blocks, 8, width), f32)
        extra["vec_mp"] = vm((members, 8, width), f32)
        extra["hs_all"] = vm((blocks, 8 * heads, 128), f32)
    else:
        q3, k3, v3 = (w.reshape(shard, heads, depth) for w in (query_weight, key_weight, value_weight))
        kv = jnp.stack([k3, v3], axis=2).reshape(shard, 2 * cols)
        out_t = jnp.pad(out_weight.T, ((0, 0), (0, 256 - cols)))
        mine = jnp.concatenate([kv, query_weight, pos_kernel, out_t, inner_weight, outer_weight.T], axis=1)
        gathered = lax.all_gather(mine, "dp", axis=0, tiled=True)[None]
        bounds = np.cumsum([0] + [full[name] for name in IN_WHOLE])
        given += [gathered[:, :, lo:hi] for lo, hi in zip(bounds[:-1], bounds[1:])]
        names = IN_BOTH + IN_WHOLE
        outs |= {name: sds((1, width, full[name]), bf16) for name in OUT_WHOLE}

    block = (members, rows, width)
    per_head = (heads, seq, 128)
    scratch = {
        "xs": vm(block, bf16), "hb": vm(block, bf16), "eb2": vm(block, bf16), "eb1": vm(block, bf16),
        "part_a": vm(block, bf16), "part_b": vm(block, bf16),
        "r1a": vm((2, rows, width), bf16), "r1b": vm((2, rows, width), bf16),
        "r2a": vm((rows, width), bf16), "r2b": vm((rows, width), bf16),
        "sxa": vm((rows, width), bf16), "sxb": vm((rows, width), bf16),
        "own_f": vm((rows, width), f32), "table": vm((2 * seq, width), bf16), "rel": vm((heads, 2 * seq, 128), bf16),
        "qa": vm(per_head, bf16), "qr": vm(per_head, bf16), "ka": vm(per_head, bf16), "va": vm(per_head, bf16),
        "q32": vm(per_head, f32), "es": vm((heads, seq, seq), bf16), "a32": vm(per_head, f32),
        "attnp": vm((seq, 256), bf16), "act": vm((members, rows, hidden), bf16),
        "slope": vm((members, rows, hidden), bf16), "igr": vm((members, rows, hidden), bf16),
        "h1": vm((rows, width), f32), "n1": vm((rows, width), f32), "e2": vm((rows, width), f32),
        "inv1": vm((rows, 128), f32), "e1": vm((rows, width), f32), "dkv": vm((heads, 128, seq), f32),
        "drt": vm((256, 2 * seq), f32), "dqkv": vm((seq, 640), bf16), "flip": vm((rows, rows), bf16),
        "qmeta": vm((seq, 128), bf16), "kmeta": vm((seq, 128), bf16), "small": vm((heads, 8, 128), f32), "per_head": vm((heads, rows, 128), f32),
        "ln": vm((8, width), f32), "ibs": vm((8, hidden), f32),
        "send_sems": pltpu.SemaphoreType.DMA((192,)), "recv_sems": pltpu.SemaphoreType.DMA((192,)),
    }
    scratch |= extra
    inside = pl.BlockSpec(memory_space=pltpu.VMEM)
    made = pl.pallas_call(
        functools.partial(layer_kernel, ring_on, [*names, *outs, *scratch]),
        out_shape=list(outs.values()),
        in_specs=[inside] * len(given),
        out_specs=[inside] * len(outs),
        scratch_shapes=list(scratch.values()),
        compiler_params=pltpu.CompilerParams(collective_id=0, has_side_effects=True, vmem_limit_bytes=67043328),
        name="layer",
    )(*given)
    made = dict(zip(outs, made))

    if ring_on:
        grads, vec, hs = made["grad_ref"], made["vec_ref"], made["hs_ref"]
    else:
        grads = jnp.concatenate([made[name][0] for name in ("dwa", "dwb", "dwo", "dwi", "dwu")], axis=1)
        grads = lax.psum_scatter(grads, "dp", scatter_dimension=0, tiled=True).astype(f32)
        vec, hs = lax.psum((made["vec_ref"], made["hs_ref"]), "dp")
        vec = jnp.concatenate([lax.psum(vec[:6], "mp"), vec[6:]], axis=0)
    small = sds((heads, depth), f32)
    line = sds((width,), f32)
    results = pl.pallas_call(
        finish_kernel,
        out_shape=[
            made["out_ref"], made["ig_ref"], *[sds((shard, cols), f32)] * 4, sds((cols, shard), f32),
            sds((shard, hidden), f32), sds((shard, hidden), f32), *[small] * 4, sds((heads, 2, depth), f32),
            sds((hidden,), f32), *[line] * 6,
        ],
        in_specs=[inside] * 5,
        out_specs=[inside] * 21,
        scratch_shapes=[vm((128, 256), f32)],
        name="finish",
    )(made["out_ref"], made["ig_ref"], grads, vec, hs)
    results = list(results)
    results[8] = results[8].T
    results[13] = jnp.transpose(results[13], (1, 0, 2))
    return tuple(results)


def solution(mesh):
    rows = P(("dp", "mp"), None)
    token = P("dp")
    placed = (
        (rows, token, token, token)
        + (P("dp", "mp"),) * 4
        + (P("mp", "dp"), P("dp", "mp"), P("mp", "dp"))
        + (P("mp", None),) * 4
        + (P(None, "mp", None), P("mp"))
        + (P(),) * 6
        + (rows,)
    )
    given = (
        (rows, rows)
        + (P("dp", "mp"),) * 4
        + (P("mp", "dp"), P("dp", "mp"), P("mp", "dp"))
        + (P("mp", None),) * 4
        + (P(None, "mp", None), P("mp"))
        + (P(),) * 6
    )
    return jax.shard_map(per_device, mesh=mesh, in_specs=placed, out_specs=given, check_vma=False)
```

profile of v0, /device:TPU:0, one launch (start us, length us, event | category | flops | bytes accessed | tf_op | source)
XLA Modules:
  0.0 156.6 jit_solution(9941845072531697812)
XLA Ops:
  0.7 152.8 %layer.1 = (bf16[256,768]{1,0:T(8,128)(2,1)}, bf16[256,768]{1,0:T(8,128)(2,1)}, f32[8,768]{1,0:T(8,128)}, f32[24,128]{1,0:T(8,128)}, f32[96,2560]{1,0:T(8,128)}) custom-call(bf16[256,768]{1,0:T(8,128)(2,1)} %refs_0_.1, bf16[256,768]{1,0:T(8,128)(2,1)} %refs_1_.1, s32[1024]{0:T(1024)} %refs_2_.1, s32[1024]{0:T(1024)} %refs_3_.1, f32[3,64]{1,0:T(4,128)} %refs_4_.1, ...), custom_call_target="tpu_custom_call" | custom-call | tf_op jit(solution)/shard_map/layer/pallas_call | solution.py:910
  153.5 2.9 %finish.1 = (bf16[256,768]{1,0:T(8,128)(2,1)}, bf16[256,768]{1,0:T(8,128)(2,1)}, f32[96,192]{1,0:T(8,128)}, f32[96,192]{1,0:T(8,128)}, f32[96,192]{1,0:T(8,128)}...) custom-call(bf16[256,768]{1,0:T(8,128)(2,1)} %get-tuple-element.47.o, ...), custom_call_target="tpu_custom_call" | custom-call | tf_op jit(solution)/shard_map/finish/pallas_call | solution.py:930
where the time goes:
time: 157 us
  Pallas kernels  156 us (99%)
    pallas_call x1, Pallas kernels, per_device(): pl.pallas_call(functools.partial(layer_kernel, ring_on, [*names, *outs, *...  153 us

commit v1 on v0

--- a/solution.py
+++ b/solution.py
@@ -35,6 +35,31 @@
     return pltpu.roll(value, 64, 1)
 
 
+class Move:
+    def __init__(self, src, dst, send_sem, recv_sem, where):
+        self.src, self.dst, self.where = src, dst, where
+        self.send_sem, self.recv_sem = send_sem, recv_sem
+
+    def described(self):
+        return pltpu.make_async_remote_copy(
+            src_ref=self.src() if callable(self.src) else self.src,
+            dst_ref=self.dst() if callable(self.dst) else self.dst,
+            send_sem=self.send_sem(),
+            recv_sem=self.recv_sem(),
+            device_id=self.where,
+            device_id_type=MESH,
+        )
+
+    def start(self):
+        self.described().start()
+
+    def wait_send(self):
+        self.described().wait_send()
+
+    def wait_recv(self):
+        self.described().wait_recv()
+
+
 class Links:
     def __init__(self, send_sems, recv_sems):
         self.send_sems = send_sems
@@ -43,14 +68,8 @@
         self.sent = []
 
     def start(self, src, dst, where):
-        copy = pltpu.make_async_remote_copy(
-            src_ref=src,
-            dst_ref=dst,
-            send_sem=self.send_sems.at[self.used],
-            recv_sem=self.recv_sems.at[self.used],
-            device_id=where,
-            device_id_type=MESH,
-        )
+        used = self.used
+        copy = Move(src, dst, lambda: self.send_sems.at[used], lambda: self.recv_sems.at[used], where)
         self.used += 1
         self.sent.append(copy)
         copy.start()
@@ -89,8 +108,12 @@
         along = lax.div(mine, 2)
         self.count = count
         self.place = (1 - row) * along + row * (count - 1 - along)
+        self.places = {offset: self.find(offset) for offset in range(-(count // 2), count // 2 + 1)}
 
     def at(self, offset):
+        return self.places[offset]
+
+    def find(self, offset):
         place = lax.rem(self.place + (offset + self.count), self.count)
         back = lax.div(place, self.count // 2)
         return (1 - back) * 2 * place + back * (2 * (self.count - 1 - place) + 1)
@@ -114,6 +137,10 @@
     ]
 
 
+def part_of(ref, *index):
+    return ref.at[index]
+
+
 class Spread:
     def __init__(self, links, ring, bufs):
         self.links, self.ring, self.bufs = links, ring, bufs
@@ -130,7 +157,7 @@
                 if s > 0 and s <= flow.hops:
                     self.moves[b, f].wait_recv()
                 if s < flow.hops:
-                    ref = buf.at[self.ring.at(-flow.sign * s), flow.rows]
+                    ref = functools.partial(part_of, buf, self.ring.at(-flow.sign * s), flow.rows)
                     self.moves[b, f] = self.links.start(ref, ref, {"dp": self.ring.at(flow.sign)})
 
     def step(self):
@@ -165,7 +192,9 @@
                         both = buf[owner, flow.rows].astype(f32) + got[flow.slot + s - 1, flow.rows].astype(f32)
                         buf[owner, flow.rows] = both.astype(bf16)
                     self.moves[b, f] = self.links.start(
-                        buf.at[owner, flow.rows], got.at[flow.slot + s, flow.rows], {"dp": self.ring.at(flow.sign)}
+                        functools.partial(part_of, buf, owner, flow.rows),
+                        functools.partial(part_of, got, flow.slot + s, flow.rows),
+                        {"dp": self.ring.at(flow.sign)},
                     )
 
     def step(self):
@@ -411,20 +440,26 @@
 
     if ring_on:
         spread_o.step()
+        spread_i.begin()
     x_b.wait_recv()
     x_f.wait_recv()
     lax.fori_loop(0, members, project, 0)
     if ring_on:
         poll(spread_o)
-        spread_i.begin()
+        spread_u.begin()
 
     wide = seq + rows
 
-    def attend(o, between=None):
+    def hooked(hooks, h):
+        for when, hook in (hooks or {}).items():
+            pl.when(h == when)(hook)
+
+    def attend(o, hooks=None):
         at = pl.ds(pl.multiple_of(o * rows, rows), rows)
         window = pl.ds(pl.multiple_of((members - 1 - o) * rows, rows), wide)
 
         def one_head(h, carry):
+            hooked(hooks, h)
             s = mm(qa[h, at, :], ka[h], NT)
             g = mm(qr[h, at, :], rel[h, window, :], NT)
             g = pltpu.roll(g, wide + 1 - rows, 1, stride=1, stride_axis=0)
@@ -437,10 +472,7 @@
             a32[h, at, :] = jnp.where(lane_of(rows) < 64, o_full * inv, inv)
             return carry
 
-        if between:
-            lax.fori_loop(0, 1, one_head, 0)
-            between()
-        lax.fori_loop(1 if between else 0, heads, one_head, 0)
+        lax.fori_loop(0, heads, one_head, 0)
         first = low_half(a32[0, at, :]) + swap(low_half(a32[1, at, :]))
         attnp[at, :128] = first.astype(bf16)
         attnp[at, 128:] = low_half(a32[2, at, :]).astype(bf16)
@@ -479,7 +511,9 @@
             self.far[x].wait_recv()
             both = self.part[across, halves[x]].astype(f32) + self.r1[1 - side, halves[x]].astype(f32)
             self.sx[halves[x]] = both.astype(bf16)
-            self.over[x] = links.start(self.sx.at[halves[x]], self.r2.at[halves[x]], to_across)
+            self.over[x] = links.start(
+                functools.partial(part_of, self.sx, halves[x]), functools.partial(part_of, self.r2, halves[x]), to_across
+            )
 
         def release(self):
             links.drain(self.far + self.near + self.over)
@@ -494,29 +528,28 @@
         return value[:part_rows], value[part_rows:]
 
     first_red = red = Scatter(part_a, r1a, r2a, sxa)
-    attend(diag)
-    if ring_on:
-        poll(spread_o, spread_i)
-        spread_u.begin()
-    attend(across)
+
+    def first_pass():
+        red.pass_on(0)
+        red.pass_on(1)
+
+    def polls(**at):
+        return {int(when[1:]): functools.partial(poll, *steppers) for when, steppers in at.items()}
+
+    attend(diag, polls(h2=(spread_o, spread_i)) if ring_on else None)
+    attend(across, polls(h1=(spread_u,), h2=(spread_o,)) if ring_on else None)
     if ring_on:
         spread_o.finish()
+        poll(spread_i)
     for x, (there, here) in enumerate(zip(split(branch_of(diag)), split(branch_of(across)))):
         red.give_diag(x, there)
         red.give_across(x, here)
-    if ring_on:
-        poll(spread_i, spread_u)
-
-    def first_pass():
-        red.pass_on(0)
-        red.pass_on(1)
-
-    attend(mate, first_pass)
+    attend(mate, {1: first_pass} | (polls(h2=(spread_u,)) if ring_on else {}))
     for x, value in enumerate(split(branch_of(mate))):
         red.give_mate(x, value)
     if ring_on:
-        poll(spread_i, spread_u)
-    attend(me)
+        poll(spread_i)
+    attend(me, polls(h2=(spread_u,)) if ring_on else None)
     for x, value in enumerate(split(branch_of(me))):
         red.give_own(x, value)
     vec_ref[...] = jnp.zeros((8, width), f32)
@@ -565,8 +598,6 @@
         spread_i.finish()
         spread_u.finish()
 
-    if ring_on:
-        poll(spread_i, spread_u)
     second_red = red = Scatter(part_b, r1b, r2b, sxb)
     stage(first_norm, ffn, second_red, weights_ready if ring_on else None)
 
@@ -630,7 +661,7 @@
     dkv[...] = jnp.zeros(dkv.shape, f32)
     drt[...] = jnp.zeros(drt.shape, f32)
 
-    def attend_back(o):
+    def attend_back(o, hooks=None):
         at = pl.ds(pl.multiple_of(o * rows, rows), rows)
         lo = pl.multiple_of((members - 1 - o) * rows, rows)
         window = pl.ds(lo, wide)
@@ -642,6 +673,7 @@
         per_head[2] = d_all[:, 128:]
 
         def one_head(h, carry):
+            hooked(hooks, h)
             d_out = per_head[h]
             kept = a32[h, at, :]
             d_out = low_half(d_out * kept[:, 64:65]).astype(bf16).astype(f32)
@@ -680,17 +712,17 @@
         dqkv[at, 384:512] = (per_head[0] + swap(per_head[1])).astype(bf16)
         dqkv[at, 512:640] = per_head[2].astype(bf16)
 
-    attend_back(me)
+    attend_back(me, polls(h2=(collect_u,)) if ring_on else None)
     g_0.beside.wait_recv()
     g_1.beside.wait_recv()
     g_0.forward()
     g_1.forward()
     if ring_on:
-        poll(spread_4, collect_u, collect_i)
-    attend_back(mate)
-    if ring_on:
-        poll(spread_4, collect_u, collect_i)
-    attend_back(across)
+        poll(spread_4, collect_i)
+    attend_back(mate, polls(h1=(spread_4,), h2=(collect_u,)) if ring_on else None)
+    if ring_on:
+        poll(spread_4, collect_i)
+    attend_back(across, polls(h1=(collect_u,), h2=(collect_i,)) if ring_on else None)
     g_0.last.wait_recv()
     g_1.last.wait_recv()
     put(dwo, mm(flat(eb1), attnp[...], TN))
@@ -701,12 +733,11 @@
             total = total + vec_all[i]
         vec_mp[me] = total
         v_a, v_b = gather_start(vec_mp)
-        poll(collect_u, collect_i)
         collect_2 = Collect(links, ring, [dwo], [r["gwo"]])
         collect_2.begin()
-    attend_back(diag)
-    if ring_on:
-        poll(collect_u, collect_i, collect_2)
+    attend_back(diag, polls(h2=(collect_2,)) if ring_on else None)
+    if ring_on:
+        poll(collect_2)
         v_b.wait_recv()
         v_f = gather_forward(vec_mp, v_a)
 

time: 157 us -> 153 us (0.975)
  Pallas kernels: 156 us -> 152 us
    pallas_call x1, Pallas kernels: 153 us -> 149 us  [per_device(): pl.pallas_call(functools.partial(layer_kernel, ring_on, [*names, *outs, *...]
where the time goes in v1:
time: 153 us; the launch traced here: 152 us
  Pallas kernels  152 us (99%)
    pallas_call x1, Pallas kernels, per_device(): pl.pallas_call(functools.partial(layer_kernel, ring_on, [*names, *outs, *...  149 us

profile of v1, /device:TPU:0, one launch (start us, length us, event | category | flops | bytes accessed | tf_op | source)
XLA Modules:
  0.0 152.4 jit_solution(16146042785536226952)
XLA Ops:
  0.7 148.7 %layer.1 = (bf16[256,768]{1,0:T(8,128)(2,1)}, bf16[256,768]{1,0:T(8,128)(2,1)}, f32[8,768]{1,0:T(8,128)}, f32[24,128]{1,0:T(8,128)}, f32[96,2560]{1,0:T(8,128)}) custom-call(bf16[256,768]{1,0:T(8,128)(2,1)} %refs_0_.1, bf16[256,768]{1,0:T(8,128)(2,1)} %refs_1_.1, s32[1024]{0:T(1024)} %refs_2_.1, s32[1024]{0:T(1024)} %refs_3_.1, f32[3,64]{1,0:T(4,128)} %refs_4_.1, ...), custom_call_target="tpu_custom_call" | custom-call | tf_op jit(solution)/shard_map/layer/pallas_call | solution.py:941
  149.4 2.9 %finish.1 = (bf16[256,768]{1,0:T(8,128)(2,1)}, bf16[256,768]{1,0:T(8,128)(2,1)}, f32[96,192]{1,0:T(8,128)}, f32[96,192]{1,0:T(8,128)}, f32[96,192]{1,0:T(8,128)}...) custom-call(bf16[256,768]{1,0:T(8,128)(2,1)} %get-tuple-element.47.o, ...), custom_call_target="tpu_custom_call" | custom-call | tf_op jit(solution)/shard_map/finish/pallas_call | solution.py:961

commit v2 on v1

--- a/solution.py
+++ b/solution.py
@@ -358,7 +358,6 @@
     kmeta_ref[...] = jnp.where(
         lane < 66, 1.0, jnp.where(lane < 68, kind, jnp.where(lane < 68 + slots, miss, 0.0))
     ).astype(bf16)
-    x_f = gather_forward(xs, x_a)
     if ring_on:
         spread_1.step()
 
@@ -375,6 +374,7 @@
     lax.fori_loop(0, ta_ref.shape[1] // 2, table_step, 0)
     if ring_on:
         spread_1.step()
+    x_f = gather_forward(xs, x_a)
     lax.fori_loop(ta_ref.shape[1] // 2, ta_ref.shape[1], table_step, 0)
 
     ri = lax.broadcasted_iota(jnp.int32, (rows, rows), 0)

time: 153 us -> 148 us (0.967)
  Pallas kernels: 152 us -> 147 us
    pallas_call x1, Pallas kernels: 149 us -> 144 us  [per_device(): pl.pallas_call(functools.partial(layer_kernel, ring_on, [*names, *outs, *...]
where the time goes in v2:
time: 148 us
  Pallas kernels  147 us (99%)
    pallas_call x1, Pallas kernels, per_device(): pl.pallas_call(functools.partial(layer_kernel, ring_on, [*names, *outs, *...  144 us

profile of v2, /device:TPU:0, one launch (start us, length us, event | category | flops | bytes accessed | tf_op | source)
XLA Modules:
  0.0 147.5 jit_solution(18429632264349071988)
XLA Ops:
  0.7 143.8 %layer.1 = (bf16[256,768]{1,0:T(8,128)(2,1)}, bf16[256,768]{1,0:T(8,128)(2,1)}, f32[8,768]{1,0:T(8,128)}, f32[24,128]{1,0:T(8,128)}, f32[96,2560]{1,0:T(8,128)}) custom-call(bf16[256,768]{1,0:T(8,128)(2,1)} %refs_0_.1, bf16[256,768]{1,0:T(8,128)(2,1)} %refs_1_.1, s32[1024]{0:T(1024)} %refs_2_.1, s32[1024]{0:T(1024)} %refs_3_.1, f32[3,64]{1,0:T(4,128)} %refs_4_.1, ...), custom_call_target="tpu_custom_call" | custom-call | tf_op jit(solution)/shard_map/layer/pallas_call | solution.py:941
  144.4 2.9 %finish.1 = (bf16[256,768]{1,0:T(8,128)(2,1)}, bf16[256,768]{1,0:T(8,128)(2,1)}, f32[96,192]{1,0:T(8,128)}, f32[96,192]{1,0:T(8,128)}, f32[96,192]{1,0:T(8,128)}...) custom-call(bf16[256,768]{1,0:T(8,128)(2,1)} %get-tuple-element.47.o, ...), custom_call_target="tpu_custom_call" | custom-call | tf_op jit(solution)/shard_map/finish/pallas_call | solution.py:961
